TPU v7x, 32 devices: a whole 2x2x4 slice. The times are simulated.
32 devices in a mesh: wide: 8 (over z, y), narrow: 4 (over x, core).
Axes of the slice: x: 2, y: 2, z: 4, core: 2. Of those that a mesh axis runs over, the one named last changes fastest.
Arguments:
- amplitudes: float32 [8, 64, 256, 256], P('wide', 'narrow'), may hold values from -6 to 6
- driver: float32 [8, 64, 256, 256], P('wide', 'narrow'), may hold values from -15 to 15
- fit_vectors: float32 [64, 1024, 256], P('narrow', 'wide'), may hold values from -0.09375 to 0.09375
- ladder_factors: float32 [2, 256, 256], P(None, 'wide'), may hold values from -0.25 to 0.25
- row_energy: float32 [8], P('wide'), may hold values from -2 to -0.3
- occupied_energy: float32 [64], P('narrow'), may hold values from -2 to -0.3
- virtual_energy: float32 [256], replicated, may hold values from 0.5 to 3
Outputs:
- updated: float32 [8, 64, 256, 256], P('wide', 'narrow')
All inputs are finite; a program needn't handle non-finite values.
Results may differ from a plain program's by a relative error of at most 0.0001.
Values sent between devices are 32-bit elements; how exact they have to be, the bound alone decides.
A program may use at most 128 MiB of HBM per device.

v0:
```python
import jax
import jax.numpy as jnp
from jax import lax
from jax.sharding import PartitionSpec as P

ITERS = 2


def ladder_part(current, full_ladder):
    highest = lax.Precision.HIGHEST
    ladder_term = jnp.zeros_like(current)
    for factor_index in range(full_ladder.shape[0]):
        factor = full_ladder[factor_index]
        left_side = jnp.einsum("ac,ijcd->ijad", factor, current, precision=highest)
        ladder_term = ladder_term + jnp.einsum(
            "ijad,bd->ijab", left_side, factor, precision=highest
        )
    return ladder_term


def advance(current, driver, denominator, full_fit, full_ladder):
    highest = lax.Precision.HIGHEST
    partial_value = jnp.einsum("ikac,kqc->iaq", current, full_fit, precision=highest)
    fitted = lax.psum(partial_value, "narrow")
    cycle_term = jnp.einsum("iaq,jqb->ijab", fitted, full_fit, precision=highest)
    ladder_term = ladder_part(current, full_ladder)
    return (driver + cycle_term + ladder_term) / denominator


def local(
    amplitudes, driver, fit_vectors, ladder_factors, row_energy, occupied_energy, virtual_energy
):
    pair_energy = virtual_energy[:, None] + virtual_energy[None, :]
    denominator = (
        pair_energy[None, None, :, :]
        - row_energy[:, None, None, None]
        - occupied_energy[None, :, None, None]
    )
    current = amplitudes
    full_fit, full_ladder = (
        lax.all_gather(fit_vectors, "wide", axis=1, tiled=True),
        lax.all_gather(ladder_factors, "wide", axis=1, tiled=True),
    )
    for iteration in range(ITERS):
        current = advance(current, driver, denominator, full_fit, full_ladder)
    return current


def solution(mesh):
    placed = (
        P("wide", "narrow", None, None),
        P("wide", "narrow", None, None),
        P("narrow", "wide", None),
        P(None, "wide", None),
        P("wide"),
        P("narrow"),
        P(),
    )
    return jax.shard_map(
        local,
        mesh=mesh,
        in_specs=placed,
        out_specs=P("wide", "narrow", None, None),
        check_vma=False,
    )
```

profile of v0, /device:TPU:0, one launch (start us, length us, event | category | flops | bytes accessed | tf_op | source)
XLA Modules:
  0.0 417.1 jit_solution(3362615845179893939)
XLA Ops:
  6.5 0.0 all-gather.2.cloned.1.call-start
  6.5 0.7 all-gather.2.cloned.1.call-update
  7.3 0.0 all-reduce.3.cloned.1.call-start
  7.9 35.5 %all_gather.7 = f32[2,256,256]{2,1,0:T(8,128)S(1)} all-gather(f32[2,32,256]{2,1,0:T(8,128)} %param.10), channel_id=1, replica_groups=mesh['wide'=8,'narrow'=4] {'wide'}, dimensions={1}, use_global_device_ids=true | all-gather | bytes 589824 | tf_op jit(solution)/shard_map/all_gather | solution.py:42
  43.4 0.0 copy-start
  43.4 8.9 %fusion.11 = f32[16,256,256]{2,1,0:T(8,128)S(1)} fusion(f32[1,16,256,256]{3,2,1,0:T(8,128)} %param.7, f32[2,256,256]{2,1,0:T(8,128)S(1)} %all_gather.7), kind=kOutput, calls=%fused_computation.15 | convolution fusion | flops 3221225472 | bytes 8650752 | tf_op jit(solution)/shard_map/ac,ijcd->ijad/dot_general | solution.py:14
  52.3 0.0 copy-done
  52.4 8.6 %fusion.13 = f32[16,256,256]{2,1,0:T(8,128)} fusion(f32[1,16,256,256]{3,2,1,0:T(8,128)S(1)} %copy-done, f32[2,256,256]{2,1,0:T(8,128)S(1)} %all_gather.7), kind=kOutput, calls=%fused_computation.17 | convolution fusion | flops 3221225472 | bytes 8650752 | tf_op jit(solution)/shard_map/ac,ijcd->ijad/dot_general | solution.py:14
  61.0 8.6 %fusion.6 = f32[16,256,256]{2,1,0:T(8,128)} fusion(f32[16,256,256]{2,1,0:T(8,128)S(1)} %fusion.11, f32[2,256,256]{2,1,0:T(8,128)S(1)} %all_gather.7), kind=kOutput, calls=%fused_computation.9 | convolution fusion | flops 3221225472 | bytes 8650752 | tf_op jit(solution)/shard_map/ijad,bd->ijab/dot_general | solution.py:15
  69.6 0.0 copy-start.2
  69.6 172.3 %all-gather.2.cloned.1.call-done = f32[16,1024,256]{2,1,0:T(8,128)} async-done(((f32[16,128,256]{2,1,0:T(8,128)}), f32[16,1024,256]{2,1,0:T(8,128)}) %all-gather.2.cloned.1.call-update) | async-done | bytes 16777232 | tf_op jit(solution)/shard_map/all_gather | solution.py:41
  241.9 18.5 %fusion.17 = f32[256,1024]{1,0:T(8,128)} fusion(f32[16,1024,256]{2,1,0:T(8,128)} %all-gather.2.cloned.1.call-done, f32[1,16,256,256]{3,2,1,0:T(8,128)} %param.7), kind=kOutput, calls=%fused_computation.21 | convolution fusion | flops 12884901888 | bytes 22020096 | tf_op jit(solution)/shard_map/ikac,kqc->iaq/dot_general | solution.py:23
  260.4 0.0 all-reduce.3.cloned.1.call-update
  260.4 0.0 all-reduce.5.cloned.1.call-start
  260.5 0.0 copy-done.2
  260.5 0.1 add_subtract_fusion
  260.6 0.0 copy-start.3
  260.6 10.9 %fusion.8 = f32[16,256,256]{2,1,0:T(8,128)} fusion(f32[16,256,256]{2,1,0:T(8,128)} %fusion.13, f32[2,256,256]{2,1,0:T(8,128)S(1)} %all_gather.7), kind=kOutput, calls=%fused_computation.11 | convolution fusion | flops 3221225472 | bytes 8650752 | tf_op jit(solution)/shard_map/ijad,bd->ijab/dot_general | solution.py:15
  271.5 23.6 %all-reduce.3.cloned.1.call-done = f32[256,1024]{1,0:T(8,128)} async-done(((f32[256,1024]{1,0:T(8,128)}), f32[256,1024]{1,0:T(8,128)}) %all-reduce.3.cloned.1.call-update) | async-done | bytes 1048592 | tf_op jit(solution)/shard_map/psum | solution.py:24
  295.1 0.0 copy-done.3
  295.1 21.2 %fusion = f32[16,256,256]{2,1,0:T(8,128)S(1)} fusion(f32[1,16,256,256]{3,2,1,0:T(8,128)} %param.8, f32[16,256,256]{2,1,0:T(8,128)} %fusion.8, f32[16,256,256]{2,1,0:T(8,128)} %fusion.6, f32[16,1024,256]{2,1,0:T(8,128)} %all-gather.2.cloned.1.call-done, f32[16]{0:T(128)S(1)} %copy-done.3, f32[256,256]{1,0:T(8,128)S(1)} %add_subtract_fusion, ...), kind=kOutput, calls=%fused_computation.2 | convolution fusion | flops 12890144768 | bytes 34865216 | tf_op jit(solution)/shard_map/iaq,jqb->ijab/dot_general | solution.py:25
  316.3 8.4 %fusion.23 = f32[16,256,256]{2,1,0:T(8,128)} fusion(f32[16,256,256]{2,1,0:T(8,128)S(1)} %fusion, f32[2,256,256]{2,1,0:T(8,128)S(1)} %all_gather.7), kind=kOutput, calls=%fused_computation.29 | convolution fusion | flops 3221225472 | bytes 8650752 | tf_op jit(solution)/shard_map/ac,ijcd->ijad/dot_general | solution.py:14
  324.7 8.8 %fusion.22 = f32[16,256,256]{2,1,0:T(8,128)} fusion(f32[16,256,256]{2,1,0:T(8,128)S(1)} %fusion, f32[2,256,256]{2,1,0:T(8,128)S(1)} %all_gather.7), kind=kOutput, calls=%fused_computation.28 | convolution fusion | flops 3221225472 | bytes 8650752 | tf_op jit(solution)/shard_map/ac,ijcd->ijad/dot_general | solution.py:14
  333.5 17.4 %convolution_bitcast_fusion = f32[256,1024]{1,0:T(8,128)} fusion(f32[16,256,256]{2,1,0:T(8,128)S(1)} %fusion, f32[16,1024,256]{2,1,0:T(8,128)} %all-gather.2.cloned.1.call-done), kind=kOutput, calls=%fused_computation.22 | convolution fusion | flops 12884901888 | bytes 22020096 | tf_op jit(solution)/shard_map/ikac,kqc->iaq/dot_general | solution.py:23
  350.9 0.0 all-reduce.5.cloned.1.call-update
  350.9 0.0 copy-start.1
  350.9 11.0 %fusion.3 = f32[16,256,256]{2,1,0:T(8,128)} fusion(f32[16,256,256]{2,1,0:T(8,128)} %fusion.22, f32[2,256,256]{2,1,0:T(8,128)S(1)} %all_gather.7), kind=kOutput, calls=%fused_computation.5 | convolution fusion | flops 3221225472 | bytes 8650752 | tf_op jit(solution)/shard_map/ijad,bd->ijab/dot_general | solution.py:15
  361.9 0.0 copy-done.1
  361.9 8.6 %fusion.1 = f32[16,256,256]{2,1,0:T(8,128)} fusion(f32[16,256,256]{2,1,0:T(8,128)S(1)} %copy-done.1, f32[2,256,256]{2,1,0:T(8,128)S(1)} %all_gather.7), kind=kOutput, calls=%fused_computation.3 | convolution fusion | flops 3221225472 | bytes 8650752 | tf_op jit(solution)/shard_map/ijad,bd->ijab/dot_general | solution.py:15
  370.5 17.3 %all-reduce.5.cloned.1.call-done = f32[256,1024]{1,0:T(8,128)} async-done(((f32[256,1024]{1,0:T(8,128)}), f32[256,1024]{1,0:T(8,128)}) %all-reduce.5.cloned.1.call-update) | async-done | bytes 1048592 | tf_op jit(solution)/shard_map/psum | solution.py:24
  387.8 22.5 %subtract_divide_fusion = f32[1,16,256,256]{3,2,1,0:T(8,128)} fusion(f32[1,16,256,256]{3,2,1,0:T(8,128)} %param.8, f32[16,256,256]{2,1,0:T(8,128)} %fusion.3, f32[16,256,256]{2,1,0:T(8,128)} %fusion.1, f32[16,1024,256]{2,1,0:T(8,128)} %all-gather.2.cloned.1.call-done, f32[16]{0:T(128)S(1)} %copy-done.3, f32[256,256]{1,0:T(8,128)S(1)} %add_subtract_fusion, ...), kind=kOutput, calls=%fused_computation | convolution fusion | flops 12890144768 | bytes 34865216 | tf_op jit(solution)/shard_map/iaq,jqb->ijab/dot_general | solution.py:25
Async XLA Ops:
  6.5 235.4 %all-gather.2.cloned.1.call-start = ((), (), s32[]{:S(2)}) async-start(), calls=%async_computation | async-start | bytes 18874368 | tf_op jit(solution)/shard_map/all_gather | solution.py:41
  7.3 287.8 %all-reduce.3.cloned.1.call-start = ((), (), s32[]{:S(2)}) async-start(), calls=%async_computation.1 | async-start | bytes 2097152 | tf_op jit(solution)/shard_map/psum | solution.py:24
  43.4 8.9 %copy-start = (f32[1,16,256,256]{3,2,1,0:T(8,128)S(1)}, f32[1,16,256,256]{3,2,1,0:T(8,128)}, u32[]{:S(2)}) copy-start(f32[1,16,256,256]{3,2,1,0:T(8,128)} %param.7) | copy-start | bytes 12582916
  69.6 190.9 %copy-start.2 = (f32[256]{0:T(256)S(1)}, f32[256]{0:T(256)}, u32[]{:S(2)}) copy-start(f32[256]{0:T(256)} %param.13) | copy-start | bytes 3076
  260.4 127.4 %all-reduce.5.cloned.1.call-start = ((), (), s32[]{:S(2)}) async-start(), calls=%async_computation.2 | async-start | bytes 2097152 | tf_op jit(solution)/shard_map/psum | solution.py:24
  260.6 34.5 %copy-start.3 = (f32[16]{0:T(128)S(1)}, f32[16]{0:T(128)}, u32[]{:S(2)}) copy-start(f32[16]{0:T(128)} %param.12) | copy-start | bytes 196
  350.9 11.0 %copy-start.1 = (f32[16,256,256]{2,1,0:T(8,128)S(1)}, f32[16,256,256]{2,1,0:T(8,128)}, u32[]{:S(2)}) copy-start(f32[16,256,256]{2,1,0:T(8,128)} %fusion.23) | copy-start | bytes 12582916
Sparse Core Ops, SparseCore 0:
  9.5 232.3 all-gather.1
  260.6 34.4 all-reduce.2
  351.0 36.7 all-reduce.4
where the time goes:
time: 425 us; the launch traced here: 417 us
  waiting for transfers between devices  214 us (50%)
  matrix products  153 us (36%)
  blocking collectives  35.5 us (8%)
  between operations  14 us (3%)
    all_gather x1, waiting for transfers between devices, local(): lax.all_gather(fit_vectors, 'wide', axis=1, tiled=True)  172 us
    dot_general x2, matrix products, advance(): jnp.einsum('iaq,jqb->ijab', fitted, full_fit, precision=highest)  43.7 us
    psum x2, waiting for transfers between devices, advance(): fitted = lax.psum(partial_value, 'narrow')  40.9 us
    dot_general x4, matrix products, ladder_part(): jnp.einsum('ijad,bd->ijab', left_side, factor, precision=highest)  39.1 us
    dot_general x2, matrix products, advance(): jnp.einsum('ikac,kqc->iaq', current, full_fit, precision=highest)  35.9 us
    all_gather x1, blocking collectives, local(): lax.all_gather(ladder_factors, 'wide', axis=1, tiled=True)  35.5 us
    dot_general x4, matrix products, ladder_part(): left_side = jnp.einsum('ac,ijcd->ijad', factor, current, precision=highest)  34.7 us
  transfers between devices with their start and end apart: 3, of which 3 were waited for; matrix products, arithmetic and copies ran while one was open for 14% of the time, Pallas kernels for 0%

commit v1 on v0

v1 whole, which is shorter than its diff:
```python
import functools

import jax
import jax.numpy as jnp
from jax import lax
from jax.experimental import pallas as pl
from jax.experimental.pallas import tpu as pltpu
from jax.sharding import PartitionSpec as P

ITERS = 2
MESH = pl.DeviceIdType.MESH
F32 = jnp.float32
BF16 = jnp.bfloat16


def split(x):
    hi = x.astype(BF16)
    lo = (x - hi.astype(F32)).astype(BF16)
    return hi, lo


def mm(a, b):
    return lax.dot_general(a, b, (((1,), (0,)), ((), ())), preferred_element_type=F32)


def mm_t(a, b):
    return lax.dot_general(a, b, (((1,), (1,)), ((), ())), preferred_element_type=F32)


def left(hi, lo):
    return jnp.concatenate([hi, hi, lo], axis=1)


def kernel(
    sizes,
    amp_hbm, drv_hbm, fit_hbm, lad_hbm, row_e, occ_e, va_ref, vb_ref,
    out_hbm,
    gath, fh, fl, amp, acc, ah, al, lad, ch, cl, part, r1, r2, fit_sum, fth, ftl,
    s_in, s_out, s_ls, s_lr, s_zs, s_zr, s_ys, s_yr, s_n1, s_n2, s_n3,
):
    W, N, K, V, QB, NL, S = sizes
    Z = W // 2
    KS = K // S
    H = V // 2
    w = lax.axis_index("wide")
    n = lax.axis_index("narrow")
    z, y = w // 2, lax.rem(w, 2)
    core = lax.rem(n, 2)
    mate = n + 1 - 2 * core
    peers = N // 2 - 1

    own_fit = pltpu.make_async_copy(fit_hbm, gath.at[z, :, pl.ds(y * QB, QB), :], s_in.at[0])
    own_fit.start()
    rows = lad_hbm.shape[1]
    own_lad = pltpu.make_async_copy(lad_hbm, lad.at[:, pl.ds(w * rows, rows), :], s_in.at[1])
    own_lad.start()
    in_amp = pltpu.make_async_copy(amp_hbm.at[0], amp, s_in.at[2])
    in_amp.start()
    in_drv = [
        pltpu.make_async_copy(drv_hbm.at[0], acc.at[it], s_in.at[3 + it]) for it in range(ITERS)
    ]
    for cp in in_drv:
        cp.start()

    bar = pltpu.get_barrier_semaphore()
    for d in range(1, W):
        pl.semaphore_signal(bar, inc=1, device_id=(lax.rem(w + d, W), n), device_id_type=MESH)
    pl.semaphore_signal(bar, inc=1, device_id=(w, mate), device_id_type=MESH)
    for d in range(1, peers + 1):
        pl.semaphore_signal(bar, inc=1, device_id=(w, lax.rem(n + 2 * d, N)), device_id_type=MESH)
    pl.semaphore_wait(bar, W - 1 + 1 + peers)

    def place(zz, yy, r):
        return gath.at[zz, pl.ds(r * KS, KS), pl.ds(yy * QB, QB), :]

    def y_copy(zz, r):
        src = place(zz, y, r)
        return pltpu.make_async_remote_copy(
            src_ref=src, dst_ref=src, send_sem=s_ys.at[zz, r], recv_sem=s_yr.at[zz, r],
            device_id=(z * 2 + 1 - y, n), device_id_type=MESH)

    def y_recv(zz, r):
        dst = place(zz, 1 - y, r)
        return pltpu.make_async_remote_copy(
            src_ref=dst, dst_ref=dst, send_sem=s_ys.at[zz, r], recv_sem=s_yr.at[zz, r],
            device_id=(z * 2 + 1 - y, n), device_id_type=MESH)

    def z_copy(zz, r, up):
        last = r // S
        src = place(zz, y + last * (1 - 2 * y), r - last * S)
        to = z + 1 if up else z - 1
        return pltpu.make_async_remote_copy(
            src_ref=src, dst_ref=src, send_sem=s_zs.at[1 if up else 0, zz, r],
            recv_sem=s_zr.at[zz, r], device_id=(to * 2 + y, n), device_id_type=MESH)

    def lad_copy(d):
        src = lad.at[:, pl.ds(w * rows, rows), :]
        return pltpu.make_async_remote_copy(
            src_ref=src, dst_ref=src, send_sem=s_ls.at[d], recv_sem=s_lr.at[d],
            device_id=(lax.rem(w + d, W), n), device_id_type=MESH)

    def lad_recv(d):
        dst = lad.at[:, pl.ds(lax.rem(w + W - d, W) * rows, rows), :]
        return pltpu.make_async_remote_copy(
            src_ref=dst, dst_ref=dst, send_sem=s_ls.at[d], recv_sem=s_lr.at[d],
            device_id=(lax.rem(w + d, W), n), device_id_type=MESH)

    own_lad.wait()
    for d in range(1, W):
        lad_copy(d).start()
    own_fit.wait()

    def begin(r, carry):
        y_copy(z, r).start()

        @pl.when(z + 1 < Z)
        def _():
            z_copy(z, r, True).start()

        @pl.when(z > 0)
        def _():
            z_copy(z, r, False).start()
        return carry

    lax.fori_loop(0, S, begin, 0)

    in_amp.wait()

    def split_amp(k, carry):
        ah[k], al[k] = split(amp[k])
        return carry

    lax.fori_loop(0, K, split_amp, 0)

    y_recv(z, 0).wait_recv()

    @pl.when(z + 1 < Z)
    def _():
        z_copy(z, S, True).start()

    @pl.when(z > 0)
    def _():
        z_copy(z, S, False).start()

    for d in range(1, W):
        lad_recv(d).wait_recv()
    for p in range(NL):
        ch[p], cl[p] = split(lad[p])
    for cp in in_drv:
        cp.wait()

    def serve(s, r):
        def arrived(zz, up):
            z_copy(zz, r, up).wait_recv()

            @pl.when((z + 1 < Z) if up else (z > 0))
            def _():
                z_copy(zz, r, up).start()

            @pl.when((r >= 1) & (r < S))
            def _():
                y_copy(zz, r).start()

        @pl.when(z - 1 - s >= 0)
        def _():
            arrived(z - 1 - s, True)

        @pl.when(z + 1 + s < Z)
        def _():
            arrived(z + 1 + s, False)

    def ladder(it, k):
        th, tl = ah[k], al[k]
        right = jnp.concatenate([th, tl, th], axis=0)
        total = acc[it, k]
        for p in range(NL):
            xh, xl = split(mm(left(ch[p], cl[p]), right))
            total = total + mm_t(left(xh, xl), jnp.concatenate([ch[p], cl[p], ch[p]], axis=1))
        acc[it, k] = total

    def slot(m):
        low = jnp.minimum(z, Z - 1 - z)
        d_in = (m + 1) // 2
        sign_in = 1 if m % 2 == 0 else -1
        sign_out = jnp.where(z < Z - 1 - z, 1, -1)
        return jnp.where(m <= 2 * low, z + sign_in * d_in, z + sign_out * (m - low))

    def fitted_k(it, zz, k, first):
        if it == 0:
            bh, bl = split(gath[zz, k])
            fh[zz, k] = bh
            fl[zz, k] = bl
        else:
            bh, bl = fh[zz, k], fl[zz, k]
        got = mm_t(left(ah[k], al[k]), jnp.concatenate([bh, bl, bh], axis=1))
        part[it, zz] = jnp.where(first, got, part[it, zz] + got)

    def need(zz, r):
        @pl.when((r >= 1))
        def _():
            y_recv(zz, r).wait_recv()

    def fitted_piece(it, zz, r):
        if it == 0:
            need(zz, r)
        for q in range(KS):
            fitted_k(it, zz, r * KS + q, (r == 0) if q == 0 else False)

    mine = pl.ds(core * H, H)
    other = pl.ds((1 - core) * H, H)

    def n1(it, zz):
        return pltpu.make_async_remote_copy(
            src_ref=part.at[it, zz, other, :], dst_ref=r1.at[it, zz],
            send_sem=s_n1.at[0, it, zz], recv_sem=s_n1.at[1, it, zz],
            device_id=(w, mate), device_id_type=MESH)

    def n2(it, zz, d):
        return pltpu.make_async_remote_copy(
            src_ref=r2.at[it, zz, 0], dst_ref=r2.at[it, zz, d],
            send_sem=s_n2.at[0, it, zz, d - 1], recv_sem=s_n2.at[1, it, zz, d - 1],
            device_id=(w, lax.rem(n + 2 * d, N)), device_id_type=MESH)

    def n3(it, zz, half):
        ref = fit_sum.at[it, zz, half, :]
        return pltpu.make_async_remote_copy(
            src_ref=ref, dst_ref=ref,
            send_sem=s_n3.at[0, it, zz], recv_sem=s_n3.at[1, it, zz],
            device_id=(w, mate), device_id_type=MESH)

    def sum1(it, zz):
        n1(it, zz).wait_recv()
        r2[it, zz, 0] = part[it, zz, mine, :] + r1[it, zz]
        for d in range(1, peers + 1):
            n2(it, zz, d).start()

    def sum2(it, zz):
        total = r2[it, zz, 0]
        for d in range(1, peers + 1):
            n2(it, zz, d).wait_recv()
            total = total + r2[it, zz, d]
        fit_sum[it, zz, mine, :] = total
        n3(it, zz, mine).start()

    def sum3(it, zz):
        n3(it, zz, other).wait_recv()
        fth[zz], ftl[zz] = split(fit_sum[it, zz])

    def whole_slot(it, m):
        zz = slot(m)

        def body(r, carry):
            fitted_piece(it, zz, r)
            return carry

        lax.fori_loop(0, S, body, 0)
        n1(it, zz).start()

    pair = va_ref[...] + vb_ref[...]
    row = row_e[0]

    def finish(it, j, last):
        total = acc[it, j]
        for zz in range(Z):
            total = total + mm(
                left(fth[zz], ftl[zz]), jnp.concatenate([fh[zz, j], fl[zz, j], fh[zz, j]], axis=0))
        new = total / ((pair - row) - occ_e[j])
        if last:
            amp[j] = new
            pltpu.make_async_copy(amp.at[j], out_hbm.at[0, j], s_out.at[j]).start()
        else:
            ah[j], al[j] = split(new)

    for s in range(Z - 1):
        def tick(r, carry, s=s):
            serve(s, r)

            @pl.when(r < S)
            def _():
                if s == 0:
                    for q in range(KS):
                        ladder(0, r * KS + q)
                else:
                    fitted_piece(0, slot(s - 1), r)
            return carry

        lax.fori_loop(0, S + 1, tick, 0)
        if s > 0:
            n1(0, slot(s - 1)).start()
    for m in range(Z - 2, Z):
        whole_slot(0, m)

    for it in range(ITERS):
        if it > 0:
            for m in range(Z):
                whole_slot(it, m)
                if m > 0:
                    sum1(it, slot(m - 1))
                if m > 1:
                    sum2(it, slot(m - 2))
            sum1(it, slot(Z - 1))

            def lad_body(k, carry, it=it):
                ladder(it, k)
                return carry

            lax.fori_loop(0, K // 2, lad_body, 0)
            sum2(it, slot(Z - 2))
            sum2(it, slot(Z - 1))
            lax.fori_loop(K // 2, K, lad_body, 0)
            for m in range(Z):
                sum3(it, slot(m))
        else:
            for m in range(Z):
                sum1(it, slot(m))
            for m in range(Z):
                sum2(it, slot(m))
            for m in range(Z):
                sum3(it, slot(m))

        def fin_body(j, carry, it=it):
            finish(it, j, it == ITERS - 1)
            return carry

        lax.fori_loop(0, K, fin_body, 0)

    def out_body(j, carry):
        pltpu.make_async_copy(amp.at[j], out_hbm.at[0, j], s_out.at[j]).wait()
        return carry

    lax.fori_loop(0, K, out_body, 0)
    for d in range(1, W):
        lad_copy(d).wait_send()

    def end_y(r, carry):
        y_copy(z, r).wait_send()
        return carry

    lax.fori_loop(0, S, end_y, 0)

    def end_z(t, carry):
        zz, r = t // (S + 1), lax.rem(t, S + 1)

        @pl.when((zz <= z) & (z + 1 < Z))
        def _():
            z_copy(zz, r, True).wait_send()

        @pl.when((zz >= z) & (z > 0))
        def _():
            z_copy(zz, r, False).wait_send()

        @pl.when((zz != z) & (r >= 1) & (r < S))
        def _():
            y_copy(zz, r).wait_send()
        return carry

    lax.fori_loop(0, Z * (S + 1), end_z, 0)

    def end_n(zz, carry):
        for it in range(ITERS):
            n1(it, zz).wait_send()
            for d in range(1, peers + 1):
                n2(it, zz, d).wait_send()
            n3(it, zz, mine).wait_send()
        return carry

    lax.fori_loop(0, Z, end_n, 0)


def solution(mesh):
    W, N = mesh.shape["wide"], mesh.shape["narrow"]
    Z = W // 2

    def local(amplitudes, driver, fit, ladder, row_e, occ_e, virt):
        K, V = amplitudes.shape[1], amplitudes.shape[2]
        QB, NL = fit.shape[1], ladder.shape[0]
        S = max(K // 2, 1)
        QP = 2 * QB
        H = V // 2
        peers = N // 2 - 1
        any_ = pl.BlockSpec(memory_space=pl.ANY)
        smem = pl.BlockSpec(memory_space=pltpu.SMEM)
        vmem = pl.BlockSpec(memory_space=pltpu.VMEM)
        dma = pltpu.SemaphoreType.DMA
        return pl.pallas_call(
            functools.partial(kernel, (W, N, K, V, QB, NL, S)),
            out_shape=jax.ShapeDtypeStruct(amplitudes.shape, F32),
            in_specs=[any_, any_, any_, any_, smem, smem, vmem, vmem],
            out_specs=any_,
            scratch_shapes=[
                pltpu.VMEM((Z, K, QP, V), F32),
                pltpu.VMEM((Z, K, QP, V), BF16),
                pltpu.VMEM((Z, K, QP, V), BF16),
                pltpu.VMEM((K, V, V), F32),
                pltpu.VMEM((ITERS, K, V, V), F32),
                pltpu.VMEM((K, V, V), BF16),
                pltpu.VMEM((K, V, V), BF16),
                pltpu.VMEM((NL, V, V), F32),
                pltpu.VMEM((NL, V, V), BF16),
                pltpu.VMEM((NL, V, V), BF16),
                pltpu.VMEM((ITERS, Z, V, QP), F32),
                pltpu.VMEM((ITERS, Z, H, QP), F32),
                pltpu.VMEM((ITERS, Z, peers + 1, H, QP), F32),
                pltpu.VMEM((ITERS, Z, V, QP), F32),
                pltpu.VMEM((Z, V, QP), BF16),
                pltpu.VMEM((Z, V, QP), BF16),
                dma((3 + ITERS,)),
                dma((K,)),
                dma((W,)),
                dma((W,)),
                dma((2, Z, S + 1)),
                dma((Z, S + 1)),
                dma((Z, S)),
                dma((Z, S)),
                dma((2, ITERS, Z)),
                dma((2, ITERS, Z, peers)),
                dma((2, ITERS, Z)),
            ],
            compiler_params=pltpu.CompilerParams(
                collective_id=0, has_side_effects=True, vmem_limit_bytes=67043328),
        )(amplitudes, driver, fit, ladder, row_e, occ_e, virt[:, None], virt[None, :])

    placed = (
        P("wide", "narrow", None, None),
        P("wide", "narrow", None, None),
        P("narrow", "wide", None),
        P(None, "wide", None),
        P("wide"),
        P("narrow"),
        P(),
    )
    return jax.shard_map(
        local,
        mesh=mesh,
        in_specs=placed,
        out_specs=P("wide", "narrow", None, None),
        check_vma=False,
    )
```

time: 425 us -> 249 us (0.59); the launches traced: 417 us -> 249 us
  Pallas kernels: 0 us -> 242 us
  waiting for transfers between devices: 214 us -> 0 us
  matrix products: 153 us -> 0 us
  blocking collectives: 35.5 us -> 0 us
  between operations: 14 us -> 0.66 us
  local copies, waits for them, and re-layouts: 0.02 us -> 6.07 us
    pallas_call x0 -> x1, Pallas kernels: none -> 242 us  [local(): pl.pallas_call(functools.partial(kernel, (W, N, K, V, QB, NL, S)), out_sh...]
    all_gather x1 -> x0, waiting for transfers between devices: 172 us -> none  [local(): lax.all_gather(fit_vectors, 'wide', axis=1, tiled=True)]
    dot_general x12 -> x0, matrix products: 153 us -> none  [the longest x2 43.7 us: advance(): jnp.einsum('iaq,jqb->ijab', fitted, full_fit, precision=highest)]
    psum x2 -> x0, waiting for transfers between devices: 40.9 us -> none  [advance(): fitted = lax.psum(partial_value, 'narrow')]
    all_gather x1 -> x0, blocking collectives: 35.5 us -> none  [local(): lax.all_gather(ladder_factors, 'wide', axis=1, tiled=True)]
    unnamed x8 -> x1, local copies, waits for them, and re-layouts: 0.02 us -> 4.6 us
  transfers between devices with their start and end apart: 3 -> 0, of which waited for: 3 -> 0; matrix products, arithmetic and copies ran while one was open for 14% -> 0% of each run, Pallas kernels for 0% -> 0%
where the time goes in v1:
time: 249 us
  Pallas kernels  242 us (97%)
  local copies, waits for them, and re-layouts  6.07 us (2%)
    pallas_call x1, Pallas kernels, local(): pl.pallas_call(functools.partial(kernel, (W, N, K, V, QB, NL, S)), out_sh...  242 us

profile of v1, /device:TPU:0, one launch (start us, length us, event | category | flops | bytes accessed | tf_op | source)
XLA Modules:
  0.0 248.9 jit_solution(13106688973647505312)
XLA Ops:
  0.7 1.5 copy.8.va_ref
  2.1 242.2 %shard_map.73 = f32[1,16,256,256]{3,2,1,0:T(8,128)} custom-call(f32[1,16,256,256]{3,2,1,0:T(8,128)} %amp_hbm.1, f32[1,16,256,256]{3,2,1,0:T(8,128)} %drv_hbm.1, f32[16,128,256]{2,1,0:T(8,128)} %fit_hbm.1, f32[2,32,256]{2,1,0:T(8,128)} %lad_hbm.1, f32[1]{0:T(128)S(6)} %copy.10.row_e, f32[16]{0:T(128)} %occ_e.1, f32[256,1]{1,0:T(8,128)} %copy.8.va_ref, ...), custom_call_target="tpu_custom_call" | custom-call | tf_op jit(solution)/shard_map/pallas_call | solution.py:385
  244.3 4.6 %copy.11 = f32[1,16,256,256]{3,2,1,0:T(8,128)} copy(f32[1,16,256,256]{3,2,1,0:T(8,128)} %shard_map.73) | data formatting | bytes 8388608

commit v2 on v1

--- a/solution.py
+++ b/solution.py
@@ -36,7 +36,7 @@
     amp_hbm, drv_hbm, fit_hbm, lad_hbm, row_e, occ_e, va_ref, vb_ref,
     out_hbm,
     gath, fh, fl, amp, acc, ah, al, lad, ch, cl, part, r1, r2, fit_sum, fth, ftl,
-    s_in, s_out, s_ls, s_lr, s_zs, s_zr, s_ys, s_yr, s_n1, s_n2, s_n3,
+    s_in, s_out, s_ls, s_lr, s_ns, s_nr, s_zs, s_zr, s_ys, s_yr, s_n1, s_n2, s_n3,
 ):
     W, N, K, V, QB, NL, S = sizes
     Z = W // 2
@@ -52,23 +52,24 @@
     own_fit = pltpu.make_async_copy(fit_hbm, gath.at[z, :, pl.ds(y * QB, QB), :], s_in.at[0])
     own_fit.start()
     rows = lad_hbm.shape[1]
-    own_lad = pltpu.make_async_copy(lad_hbm, lad.at[:, pl.ds(w * rows, rows), :], s_in.at[1])
+    D = lad.shape[2]
+    share = lax.rem(n, D)
+    rows_part = rows // D
+    own_lad = pltpu.make_async_copy(
+        lad_hbm.at[:, pl.ds(pl.multiple_of(share * rows_part, rows_part), rows_part), :],
+        lad.at[:, w, share], s_in.at[1])
     own_lad.start()
     in_amp = pltpu.make_async_copy(amp_hbm.at[0], amp, s_in.at[2])
-    in_amp.start()
     in_drv = [
         pltpu.make_async_copy(drv_hbm.at[0], acc.at[it], s_in.at[3 + it]) for it in range(ITERS)
     ]
-    for cp in in_drv:
-        cp.start()
 
     bar = pltpu.get_barrier_semaphore()
     for d in range(1, W):
         pl.semaphore_signal(bar, inc=1, device_id=(lax.rem(w + d, W), n), device_id_type=MESH)
-    pl.semaphore_signal(bar, inc=1, device_id=(w, mate), device_id_type=MESH)
-    for d in range(1, peers + 1):
-        pl.semaphore_signal(bar, inc=1, device_id=(w, lax.rem(n + 2 * d, N)), device_id_type=MESH)
-    pl.semaphore_wait(bar, W - 1 + 1 + peers)
+    for d in range(1, N):
+        pl.semaphore_signal(bar, inc=1, device_id=(w, lax.rem(n + d, N)), device_id_type=MESH)
+    pl.semaphore_wait(bar, W + N - 2)
 
     def place(zz, yy, r):
         return gath.at[zz, pl.ds(r * KS, KS), pl.ds(yy * QB, QB), :]
@@ -94,35 +95,47 @@
             recv_sem=s_zr.at[zz, r], device_id=(to * 2 + y, n), device_id_type=MESH)
 
     def lad_copy(d):
-        src = lad.at[:, pl.ds(w * rows, rows), :]
+        src = lad.at[:, w, share]
         return pltpu.make_async_remote_copy(
             src_ref=src, dst_ref=src, send_sem=s_ls.at[d], recv_sem=s_lr.at[d],
             device_id=(lax.rem(w + d, W), n), device_id_type=MESH)
 
     def lad_recv(d):
-        dst = lad.at[:, pl.ds(lax.rem(w + W - d, W) * rows, rows), :]
+        dst = lad.at[:, lax.rem(w + W - d, W), share]
         return pltpu.make_async_remote_copy(
             src_ref=dst, dst_ref=dst, send_sem=s_ls.at[d], recv_sem=s_lr.at[d],
             device_id=(lax.rem(w + d, W), n), device_id_type=MESH)
 
+    own_fit.wait()
     own_lad.wait()
+
+    def lad_spread(d, mine):
+        part_of = share if mine else lax.rem(share + D - d, D)
+        ref = lad.at[:, :, part_of]
+        return pltpu.make_async_remote_copy(
+            src_ref=ref, dst_ref=ref, send_sem=s_ns.at[d], recv_sem=s_nr.at[d],
+            device_id=(w, n - share + lax.rem(share + d, D)), device_id_type=MESH)
+
+
+    def begin(r, carry):
+        y_copy(z, r).start()
+
+        @pl.when(z + 1 < Z)
+        def _():
+            z_copy(z, r, True).start()
+
+        @pl.when(z > 0)
+        def _():
+            z_copy(z, r, False).start()
+        return carry
+
+    begin(0, 0)
     for d in range(1, W):
         lad_copy(d).start()
-    own_fit.wait()
-
-    def begin(r, carry):
-        y_copy(z, r).start()
-
-        @pl.when(z + 1 < Z)
-        def _():
-            z_copy(z, r, True).start()
-
-        @pl.when(z > 0)
-        def _():
-            z_copy(z, r, False).start()
-        return carry
-
-    lax.fori_loop(0, S, begin, 0)
+    lax.fori_loop(1, S, begin, 0)
+    in_amp.start()
+    for cp in in_drv:
+        cp.start()
 
     in_amp.wait()
 
@@ -144,8 +157,12 @@
 
     for d in range(1, W):
         lad_recv(d).wait_recv()
+    for d in range(1, D):
+        lad_spread(d, True).start()
+    for d in range(1, D):
+        lad_spread(d, False).wait_recv()
     for p in range(NL):
-        ch[p], cl[p] = split(lad[p])
+        ch[p], cl[p] = split(lad[p].reshape(V, V))
     for cp in in_drv:
         cp.wait()
 
@@ -259,17 +276,45 @@
     pair = va_ref[...] + vb_ref[...]
     row = row_e[0]
 
-    def finish(it, j, last):
+    def cycle(zz, j):
+        return mm(
+            left(fth[zz], ftl[zz]), jnp.concatenate([fh[zz, j], fl[zz, j], fh[zz, j]], axis=0))
+
+    def cycles(it, slots):
+        def body(j, carry):
+            total = acc[it, j]
+            for m in slots:
+                total = total + cycle(slot(m), j)
+            acc[it, j] = total
+            return carry
+
+        lax.fori_loop(0, K, body, 0)
+
+    def finish(it, j, slots, last):
         total = acc[it, j]
-        for zz in range(Z):
-            total = total + mm(
-                left(fth[zz], ftl[zz]), jnp.concatenate([fh[zz, j], fl[zz, j], fh[zz, j]], axis=0))
+        for m in slots:
+            total = total + cycle(slot(m), j)
         new = total / ((pair - row) - occ_e[j])
         if last:
             amp[j] = new
             pltpu.make_async_copy(amp.at[j], out_hbm.at[0, j], s_out.at[j]).start()
         else:
             ah[j], al[j] = split(new)
+
+    def finish_all(it, slots):
+        def body(j, carry):
+            finish(it, j, slots, it == ITERS - 1)
+            return carry
+
+        lax.fori_loop(0, K, body, 0)
+
+    def sums(it, slots):
+        for m in slots:
+            sum1(it, slot(m))
+        for m in slots:
+            sum2(it, slot(m))
+        for m in slots:
+            sum3(it, slot(m))
 
     for s in range(Z - 1):
         def tick(r, carry, s=s):
@@ -282,47 +327,59 @@
                         ladder(0, r * KS + q)
                 else:
                     fitted_piece(0, slot(s - 1), r)
+            if s > 1:
+                zz = slot(s - 2)
+                for at, stage in ((0, sum1), (S // 2, sum2), (S, sum3)):
+                    @pl.when(r == at)
+                    def _(stage=stage, zz=zz):
+                        stage(0, zz)
             return carry
 
         lax.fori_loop(0, S + 1, tick, 0)
         if s > 0:
             n1(0, slot(s - 1)).start()
-    for m in range(Z - 2, Z):
-        whole_slot(0, m)
-
-    for it in range(ITERS):
-        if it > 0:
-            for m in range(Z):
-                whole_slot(it, m)
-                if m > 0:
-                    sum1(it, slot(m - 1))
-                if m > 1:
-                    sum2(it, slot(m - 2))
-            sum1(it, slot(Z - 1))
-
-            def lad_body(k, carry, it=it):
-                ladder(it, k)
-                return carry
-
-            lax.fori_loop(0, K // 2, lad_body, 0)
-            sum2(it, slot(Z - 2))
-            sum2(it, slot(Z - 1))
-            lax.fori_loop(K // 2, K, lad_body, 0)
-            for m in range(Z):
-                sum3(it, slot(m))
-        else:
-            for m in range(Z):
-                sum1(it, slot(m))
-            for m in range(Z):
-                sum2(it, slot(m))
-            for m in range(Z):
-                sum3(it, slot(m))
-
-        def fin_body(j, carry, it=it):
-            finish(it, j, it == ITERS - 1)
+    summed = max(Z - 3, 0)
+    if Z > 1:
+        whole_slot(0, Z - 2)
+    if summed > 0:
+        cycles(0, range(summed))
+    sums(0, range(summed, Z - 1))
+    if Z > 1:
+        cycles(0, range(summed, Z - 1))
+    whole_slot(0, Z - 1)
+    sums(0, [Z - 1])
+    finish_all(0, [Z - 1])
+
+    for it in range(1, ITERS):
+        for m in range(Z):
+            whole_slot(it, m)
+            if m > 0:
+                sum1(it, slot(m - 1))
+
+        def lad_body(k, carry, it=it):
+            ladder(it, k)
             return carry
 
-        lax.fori_loop(0, K, fin_body, 0)
+        half = Z // 2
+        lax.fori_loop(0, K // 4, lad_body, 0)
+        sum1(it, slot(Z - 1))
+        lax.fori_loop(K // 4, K - K // 4, lad_body, 0)
+        for m in range(half):
+            sum2(it, slot(m))
+        lax.fori_loop(K - K // 4, K, lad_body, 0)
+        for m in range(half):
+            sum3(it, slot(m))
+        if half > 0:
+            cycles(it, range(half))
+        for m in range(half, Z - 1):
+            sum2(it, slot(m))
+        for m in range(half, Z - 1):
+            sum3(it, slot(m))
+        if half < Z - 1:
+            cycles(it, range(half, Z - 1))
+        sum2(it, slot(Z - 1))
+        sum3(it, slot(Z - 1))
+        finish_all(it, [Z - 1])
 
     def out_body(j, carry):
         pltpu.make_async_copy(amp.at[j], out_hbm.at[0, j], s_out.at[j]).wait()
@@ -331,6 +388,8 @@
     lax.fori_loop(0, K, out_body, 0)
     for d in range(1, W):
         lad_copy(d).wait_send()
+    for d in range(1, D):
+        lad_spread(d, True).wait_send()
 
     def end_y(r, carry):
         y_copy(z, r).wait_send()
@@ -376,6 +435,10 @@
         QB, NL = fit.shape[1], ladder.shape[0]
         S = max(K // 2, 1)
         QP = 2 * QB
+        rows = ladder.shape[1]
+        D = 1
+        while N % (2 * D) == 0 and rows % (16 * D) == 0:
+            D *= 2
         H = V // 2
         peers = N // 2 - 1
         any_ = pl.BlockSpec(memory_space=pl.ANY)
@@ -395,7 +458,7 @@
                 pltpu.VMEM((ITERS, K, V, V), F32),
                 pltpu.VMEM((K, V, V), BF16),
                 pltpu.VMEM((K, V, V), BF16),
-                pltpu.VMEM((NL, V, V), F32),
+                pltpu.VMEM((NL, W, D, rows // D, V), F32),
                 pltpu.VMEM((NL, V, V), BF16),
                 pltpu.VMEM((NL, V, V), BF16),
                 pltpu.VMEM((ITERS, Z, V, QP), F32),
@@ -408,6 +471,8 @@
                 dma((K,)),
                 dma((W,)),
                 dma((W,)),
+                dma((D,)),
+                dma((D,)),
                 dma((2, Z, S + 1)),
                 dma((Z, S + 1)),
                 dma((Z, S)),

time: 249 us -> 251 us (level)
  no operation moved by 1% of the time
where the time goes in v2:
time: 251 us; the launch traced here: 250 us
  Pallas kernels  243 us (97%)
  local copies, waits for them, and re-layouts  6.07 us (2%)
    pallas_call x1, Pallas kernels, local(): pl.pallas_call(functools.partial(kernel, (W, N, K, V, QB, NL, S)), out_sh...  243 us

profile of v2, /device:TPU:0, one launch (start us, length us, event | category | flops | bytes accessed | tf_op | source)
XLA Modules:
  0.0 249.9 jit_solution(17335775266652655857)
XLA Ops:
  0.7 1.5 copy.8.va_ref
  2.1 243.2 %shard_map.73 = f32[1,16,256,256]{3,2,1,0:T(8,128)} custom-call(f32[1,16,256,256]{3,2,1,0:T(8,128)} %amp_hbm.1, f32[1,16,256,256]{3,2,1,0:T(8,128)} %drv_hbm.1, f32[16,128,256]{2,1,0:T(8,128)} %fit_hbm.1, f32[2,32,256]{2,1,0:T(8,128)} %lad_hbm.1, f32[1]{0:T(128)S(6)} %copy.10.row_e, f32[16]{0:T(128)} %occ_e.1, f32[256,1]{1,0:T(8,128)} %copy.8.va_ref, ...), custom_call_target="tpu_custom_call" | custom-call | tf_op jit(solution)/shard_map/pallas_call | solution.py:448
  245.3 4.6 %copy.11 = f32[1,16,256,256]{3,2,1,0:T(8,128)} copy(f32[1,16,256,256]{3,2,1,0:T(8,128)} %shard_map.73) | data formatting | bytes 8388608

commit v3 on v1

--- a/solution.py
+++ b/solution.py
@@ -36,7 +36,7 @@
     amp_hbm, drv_hbm, fit_hbm, lad_hbm, row_e, occ_e, va_ref, vb_ref,
     out_hbm,
     gath, fh, fl, amp, acc, ah, al, lad, ch, cl, part, r1, r2, fit_sum, fth, ftl,
-    s_in, s_out, s_ls, s_lr, s_zs, s_zr, s_ys, s_yr, s_n1, s_n2, s_n3,
+    s_in, s_out, s_ls, s_lr, s_ns, s_nr, s_zs, s_zr, s_ys, s_yr, s_n1, s_n2, s_n3,
 ):
     W, N, K, V, QB, NL, S = sizes
     Z = W // 2
@@ -52,23 +52,24 @@
     own_fit = pltpu.make_async_copy(fit_hbm, gath.at[z, :, pl.ds(y * QB, QB), :], s_in.at[0])
     own_fit.start()
     rows = lad_hbm.shape[1]
-    own_lad = pltpu.make_async_copy(lad_hbm, lad.at[:, pl.ds(w * rows, rows), :], s_in.at[1])
+    D = lad.shape[2]
+    share = lax.rem(n, D)
+    rows_part = rows // D
+    own_lad = pltpu.make_async_copy(
+        lad_hbm.at[:, pl.ds(pl.multiple_of(share * rows_part, rows_part), rows_part), :],
+        lad.at[:, w, share], s_in.at[1])
     own_lad.start()
     in_amp = pltpu.make_async_copy(amp_hbm.at[0], amp, s_in.at[2])
-    in_amp.start()
     in_drv = [
         pltpu.make_async_copy(drv_hbm.at[0], acc.at[it], s_in.at[3 + it]) for it in range(ITERS)
     ]
-    for cp in in_drv:
-        cp.start()
 
     bar = pltpu.get_barrier_semaphore()
     for d in range(1, W):
         pl.semaphore_signal(bar, inc=1, device_id=(lax.rem(w + d, W), n), device_id_type=MESH)
-    pl.semaphore_signal(bar, inc=1, device_id=(w, mate), device_id_type=MESH)
-    for d in range(1, peers + 1):
-        pl.semaphore_signal(bar, inc=1, device_id=(w, lax.rem(n + 2 * d, N)), device_id_type=MESH)
-    pl.semaphore_wait(bar, W - 1 + 1 + peers)
+    for d in range(1, N):
+        pl.semaphore_signal(bar, inc=1, device_id=(w, lax.rem(n + d, N)), device_id_type=MESH)
+    pl.semaphore_wait(bar, W + N - 2)
 
     def place(zz, yy, r):
         return gath.at[zz, pl.ds(r * KS, KS), pl.ds(yy * QB, QB), :]
@@ -94,35 +95,47 @@
             recv_sem=s_zr.at[zz, r], device_id=(to * 2 + y, n), device_id_type=MESH)
 
     def lad_copy(d):
-        src = lad.at[:, pl.ds(w * rows, rows), :]
+        src = lad.at[:, w, share]
         return pltpu.make_async_remote_copy(
             src_ref=src, dst_ref=src, send_sem=s_ls.at[d], recv_sem=s_lr.at[d],
             device_id=(lax.rem(w + d, W), n), device_id_type=MESH)
 
     def lad_recv(d):
-        dst = lad.at[:, pl.ds(lax.rem(w + W - d, W) * rows, rows), :]
+        dst = lad.at[:, lax.rem(w + W - d, W), share]
         return pltpu.make_async_remote_copy(
             src_ref=dst, dst_ref=dst, send_sem=s_ls.at[d], recv_sem=s_lr.at[d],
             device_id=(lax.rem(w + d, W), n), device_id_type=MESH)
 
+    own_fit.wait()
     own_lad.wait()
+
+    def lad_spread(d, mine):
+        part_of = share if mine else lax.rem(share + D - d, D)
+        ref = lad.at[:, :, part_of]
+        return pltpu.make_async_remote_copy(
+            src_ref=ref, dst_ref=ref, send_sem=s_ns.at[d], recv_sem=s_nr.at[d],
+            device_id=(w, n - share + lax.rem(share + d, D)), device_id_type=MESH)
+
+
+    def begin(r, carry):
+        y_copy(z, r).start()
+
+        @pl.when(z + 1 < Z)
+        def _():
+            z_copy(z, r, True).start()
+
+        @pl.when(z > 0)
+        def _():
+            z_copy(z, r, False).start()
+        return carry
+
+    begin(0, 0)
     for d in range(1, W):
         lad_copy(d).start()
-    own_fit.wait()
-
-    def begin(r, carry):
-        y_copy(z, r).start()
-
-        @pl.when(z + 1 < Z)
-        def _():
-            z_copy(z, r, True).start()
-
-        @pl.when(z > 0)
-        def _():
-            z_copy(z, r, False).start()
-        return carry
-
-    lax.fori_loop(0, S, begin, 0)
+    lax.fori_loop(1, S, begin, 0)
+    in_amp.start()
+    for cp in in_drv:
+        cp.start()
 
     in_amp.wait()
 
@@ -144,8 +157,12 @@
 
     for d in range(1, W):
         lad_recv(d).wait_recv()
+    for d in range(1, D):
+        lad_spread(d, True).start()
+    for d in range(1, D):
+        lad_spread(d, False).wait_recv()
     for p in range(NL):
-        ch[p], cl[p] = split(lad[p])
+        ch[p], cl[p] = split(lad[p].reshape(V, V))
     for cp in in_drv:
         cp.wait()
 
@@ -331,6 +348,8 @@
     lax.fori_loop(0, K, out_body, 0)
     for d in range(1, W):
         lad_copy(d).wait_send()
+    for d in range(1, D):
+        lad_spread(d, True).wait_send()
 
     def end_y(r, carry):
         y_copy(z, r).wait_send()
@@ -376,6 +395,10 @@
         QB, NL = fit.shape[1], ladder.shape[0]
         S = max(K // 2, 1)
         QP = 2 * QB
+        rows = ladder.shape[1]
+        D = 1
+        while N % (2 * D) == 0 and rows % (16 * D) == 0:
+            D *= 2
         H = V // 2
         peers = N // 2 - 1
         any_ = pl.BlockSpec(memory_space=pl.ANY)
@@ -395,7 +418,7 @@
                 pltpu.VMEM((ITERS, K, V, V), F32),
                 pltpu.VMEM((K, V, V), BF16),
                 pltpu.VMEM((K, V, V), BF16),
-                pltpu.VMEM((NL, V, V), F32),
+                pltpu.VMEM((NL, W, D, rows // D, V), F32),
                 pltpu.VMEM((NL, V, V), BF16),
                 pltpu.VMEM((NL, V, V), BF16),
                 pltpu.VMEM((ITERS, Z, V, QP), F32),
@@ -408,6 +431,8 @@
                 dma((K,)),
                 dma((W,)),
                 dma((W,)),
+                dma((D,)),
+                dma((D,)),
                 dma((2, Z, S + 1)),
                 dma((Z, S + 1)),
                 dma((Z, S)),

time: 249 us -> 244 us (0.980)
  Pallas kernels: 242 us -> 237 us
    pallas_call x1, Pallas kernels: 242 us -> 237 us  [local(): pl.pallas_call(functools.partial(kernel, (W, N, K, V, QB, NL, S)), out_sh...]
where the time goes in v3:
time: 244 us
  Pallas kernels  237 us (97%)
  local copies, waits for them, and re-layouts  6.07 us (2%)
    pallas_call x1, Pallas kernels, local(): pl.pallas_call(functools.partial(kernel, (W, N, K, V, QB, NL, S)), out_sh...  237 us

profile of v3, /device:TPU:0, one launch (start us, length us, event | category | flops | bytes accessed | tf_op | source)
XLA Modules:
  0.0 243.8 jit_solution(6622016423106343619)
XLA Ops:
  0.7 1.5 copy.8.va_ref
  2.1 237.1 %shard_map.73 = f32[1,16,256,256]{3,2,1,0:T(8,128)} custom-call(f32[1,16,256,256]{3,2,1,0:T(8,128)} %amp_hbm.1, f32[1,16,256,256]{3,2,1,0:T(8,128)} %drv_hbm.1, f32[16,128,256]{2,1,0:T(8,128)} %fit_hbm.1, f32[2,32,256]{2,1,0:T(8,128)} %lad_hbm.1, f32[1]{0:T(128)S(6)} %copy.10.row_e, f32[16]{0:T(128)} %occ_e.1, f32[256,1]{1,0:T(8,128)} %copy.8.va_ref, ...), custom_call_target="tpu_custom_call" | custom-call | tf_op jit(solution)/shard_map/pallas_call | solution.py:408
  239.2 4.6 %copy.11 = f32[1,16,256,256]{3,2,1,0:T(8,128)} copy(f32[1,16,256,256]{3,2,1,0:T(8,128)} %shard_map.73) | data formatting | bytes 8388608
